TPU v7x, 256 devices: a whole 4x4x8 slice. The times are simulated.
256 devices in a mesh: batch: 2 (over x_hi), head: 8 (over y, x_lo), blk: 16 (over z, core).
Axes of the slice: x: 4 (x_hi: 2, x_lo: 2; x = x_hi * 2 + x_lo), y: 4, z: 8, core: 2. Of those that a mesh axis runs over, the one named last changes fastest.
Arguments:
- tokens: bfloat16 [32, 2048, 1024], P(('batch', 'blk'), 'head'), parts along dimension 0, may hold values from -10.5 to 10.5
- proj_weight: bfloat16 [1024, 3072], replicated, may hold values from -0.1875 to 0.1875
- out_weight: bfloat16 [1024, 1024], replicated, may hold values from -1.5 to 1.5
- pattern: int32 [512, 16], P(('batch', 'blk')), parts along dimension 0, may hold values from 0 to 255, as said below
Outputs:
- mixed_out: bfloat16 [32, 2048, 1024], P(('batch', 'blk'), 'head'), parts along dimension 0
There are 2 independent parts, one for each index of `batch`. A program takes and returns all parts, laid end to end along the dimension named above; an argument that names none is the same for every part. Nothing has to cross between parts.
Inputs may be any that keep to these rules, and one draw needn't show every extreme that they name: `pattern`: row i lists first 6 distinct blocks j with |j - i| <= 8, among them i itself, then 10 distinct summary blocks j (j % 16 >= 12) with |j - i| > 8. Every row with 8 <= i < 248 lists i - 8 and i + 8.
All inputs are finite; a program needn't handle non-finite values.
Results may differ from a plain program's by a relative error of at most 0.0095.
Values may be sent and summed in bfloat16 or wider, within the bound.
A program may use at most 128 MiB of HBM per device.

v0:
```python
import jax
import jax.numpy as jnp
from jax import lax
from jax.sharding import PartitionSpec as P

D = 1024
H = 16
HD = 64
BLK = 128
TOK_DEV = 2048
SB = 16
KSEL = 16


def on_device(tokens, proj_weight, out_weight, pattern):
    heads_axis = lax.axis_size("head")
    local_heads = H // heads_axis
    head_width = local_heads * HD
    col_width = local_heads * 3 * HD
    own_rows = tokens[0]
    local_tokens = own_rows.shape[0]
    start_col = lax.axis_index("head") * col_width
    columns = lax.dynamic_slice_in_dim(proj_weight, start_col, col_width, 1)
    columns = columns.reshape(D, local_heads, 3, HD).transpose(0, 2, 1, 3).reshape(D, col_width)
    projected = jnp.dot(
        lax.all_gather(own_rows, "head", axis=0, tiled=True),
        columns,
        preferred_element_type=jnp.float32,
    ).astype(jnp.bfloat16)
    queries = projected[:, :head_width]
    key_value = projected[:, head_width:]
    source = lax.all_gather(key_value, "blk", axis=0, tiled=True)
    source_blocks = source.reshape(-1, BLK, 2 * head_width)
    group_size = 4
    group_count = SB // group_size
    query_groups = queries.reshape(group_count, group_size, BLK, head_width)
    position_groups = pattern.reshape(group_count, group_size, KSEL)
    score_scale = HD ** (-0.5)
    lane_head = lax.broadcasted_iota(jnp.int32, (1, 1, head_width), 2) // HD

    def attend(operands):
        query_group, positions = operands
        picked = source_blocks[positions].reshape(group_size, KSEL * BLK, 2 * head_width)
        key_rows = picked[:, :, :head_width]
        value_rows = picked[:, :, head_width:]
        total = jnp.zeros((group_size, BLK, head_width), jnp.float32)
        for which in range(local_heads):
            inside = lane_head == which
            masked = jnp.where(inside, query_group, jnp.zeros_like(query_group))
            scores = (
                jnp.einsum("gqc,gkc->gqk", masked, key_rows, preferred_element_type=jnp.float32)
                * score_scale
            )
            row_max = jnp.max(scores, axis=-1, keepdims=True)
            raised = jnp.exp(scores - row_max)
            weights = (raised / jnp.sum(raised, axis=-1, keepdims=True)).astype(jnp.bfloat16)
            product = jnp.einsum(
                "gqk,gkc->gqc", weights, value_rows, preferred_element_type=jnp.float32
            )
            total = total + jnp.where(inside, product, 0.0)
        return total.astype(jnp.bfloat16)

    attended = lax.map(attend, (query_groups, position_groups))
    attended = attended.reshape(TOK_DEV, head_width)
    token_heads = lax.all_to_all(attended, "head", split_axis=0, concat_axis=1, tiled=True)
    mixed_out = jnp.dot(token_heads, out_weight, preferred_element_type=jnp.float32).astype(
        jnp.bfloat16
    )
    return mixed_out.reshape(1, local_tokens, D)


def solution(mesh):
    return jax.shard_map(
        on_device,
        mesh=mesh,
        in_specs=(P(("batch", "blk"), "head", None), P(), P(), P(("batch", "blk"), None)),
        out_specs=P(("batch", "blk"), "head", None),
        check_vma=False,
    )
```

profile of v0, /device:TPU:6, one launch (start us, length us, event | category | flops | bytes accessed | tf_op | source)
XLA Modules:
  0.0 346.7 jit_solution(8824220184311968826)
XLA Ops:
  6.5 0.0 copy-start
  6.5 0.0 all-gather.6.cloned.1.call-start
  6.5 0.7 all-gather.6.cloned.1.call-update
  7.3 0.0 all-gather.4.cloned.1.call-start
  7.3 1.2 constant_dynamic-slice_fusion
  8.5 1.2 copy.18
  9.7 1.2 copy.12
  10.9 93.8 %all-gather.6.cloned.1.call-done = bf16[1,2048,1024]{2,1,0:T(8,128)(2,1)} async-done(((bf16[1,256,1024]{2,1,0:T(8,128)(2,1)}), bf16[1,2048,1024]{2,1,0:T(8,128)(2,1)}) %all-gather.6.cloned.1.call-update) | async-done | bytes 4194320 | tf_op jit(solution)/shard_map/all_gather | solution.py:26
  104.6 4.0 %fusion.111 = bf16[2048,384]{0,1:T(8,128)(2,1)S(1)} fusion(bf16[1024,384]{0,1:T(8,128)(2,1)S(1)} %bitcast.86, bf16[1,2048,1024]{2,1,0:T(8,128)(2,1)} %all-gather.6.cloned.1.call-done), kind=kOutput, calls=%fused_computation.67 | convolution fusion | flops 1611399168 | bytes 6553600 | tf_op jit(solution)/shard_map/dot_general | solution.py:25
  108.7 1.1 copy-done.1
  109.8 1.1 slice.23
  110.9 0.0 all-gather.4.cloned.1.call-update
  110.9 1.1 slice.22
  112.0 0.3 copy.16
  112.3 94.9 %all-gather.4.cloned.1.call-done = bf16[32768,256]{0,1:T(8,128)(2,1)} async-done(((bf16[2048,256]{0,1:T(8,128)(2,1)}), bf16[32768,256]{0,1:T(8,128)(2,1)}) %all-gather.4.cloned.1.call-update) | async-done | bytes 16777232 | tf_op jit(solution)/shard_map/all_gather | solution.py:32
  207.2 22.4 %copy.17 = bf16[32768,256]{1,0:T(8,128)(2,1)} copy(bf16[32768,256]{0,1:T(8,128)(2,1)} %all-gather.4.cloned.1.call-done) | data formatting | bytes 33554432
  229.6 93.5 %while.12 = (s32[]{:T(128)}, bf16[4,4,128,128]{3,2,1,0:T(8,128)(2,1)}, bf16[4,4,128,128]{3,2,1,0:T(8,128)(2,1)S(1)}, s32[4,4,16]{2,1,0:T(4,128)}, bf16[256,128,256]{2,1,0:T(8,128)(2,1)}, /*index=5*/s32[]{:T(128)}) while((s32[]{:T(128)}, bf16[4,4,128,128]{3,2,1,0:T(8,128)(2,1)}, bf16[4,4,128,128]{3,2,1,0:T(8,128)(2,1)S(1)}, ...), condition=%wide.region_5.6_spmd.clone.clone, body=%wide.region_0.5_spmd.clone.clone.sunk | while | flops 1625828864 | bytes 22169436 | solution.py:63
  229.6 0.7 compare_select_fusion.2
  230.3 0.1 reshape.157
  230.4 8.5 %gather_fusion = bf16[64,128,256]{2,1,0:T(8,128)(2,1)} fusion(bf16[256,128,256]{2,1,0:T(8,128)(2,1)} %get-tuple-element.155, s32[1024]{0:T(1024)S(1)} %pad_clamp_fusion.2), kind=kCustom, calls=%fused_computation.clone.clone.1 | custom fusion | bytes 8388864 | tf_op jit(solution)/shard_map/while/body/eval_jaxpr/gather | solution.py:43
  238.9 2.9 fusion.146
  241.8 2.9 fusion.144
  244.7 3.8 %fusion.145 = f32[4,128,128]{2,1,0:T(8,128)S(1)} fusion(bf16[4,2048,256]{2,1,0:T(8,128)(2,1)} %bitcast.80, f32[4,128]{1,0:T(4,128)S(1)} %fusion.144, pred[128]{0:T(512)(128)(4,1)S(1)} %get-tuple-element.137, bf16[4,4,128,128]{3,2,1,0:T(8,128)(2,1)S(1)} %get-tuple-element.153, s32[]{:T(128)S(6)} %copy.22), kind=kOutput, calls=%fused_computation.25.clone.1 | convolution fusion | flops 541198848 | bytes 4590596 | tf_op jit(solution)/shard_map/while/body/eval_jaxpr/gqk,gkc->gqc/dot_general | solution.py:57
  248.5 4.5 %fusion.147 = bf16[4,4,128,128]{3,2,1,0:T(8,128)(2,1)} fusion(bf16[4,4,128,128]{3,2,1,0:T(8,128)(2,1)} %get-tuple-element.146, s32[]{:T(128)S(6)} %copy.22, f32[4,128,128]{2,1,0:T(8,128)S(1)} %fusion.145, bf16[4,2048,256]{2,1,0:T(8,128)(2,1)} %bitcast.81, f32[4,128]{1,0:T(4,128)S(1)} %fusion.146, pred[128]{0:T(512)(128)(4,1)S(1)} %get-tuple-element.138, ...), kind=kOutput, calls=%fused_computation.27.clone.1 | convolution fusion | flops 541329920 | bytes 4722688 | tf_op jit(solution)/shard_map/while/body/eval_jaxpr/gqk,gkc->gqc/dot_general | solution.py:57
  252.9 0.7 compare_select_fusion.2
  253.6 0.1 reshape.157
  253.7 8.5 %gather_fusion = bf16[64,128,256]{2,1,0:T(8,128)(2,1)} fusion(bf16[256,128,256]{2,1,0:T(8,128)(2,1)} %get-tuple-element.155, s32[1024]{0:T(1024)S(1)} %pad_clamp_fusion.2), kind=kCustom, calls=%fused_computation.clone.clone.1 | custom fusion | bytes 8388864 | tf_op jit(solution)/shard_map/while/body/eval_jaxpr/gather | solution.py:43
  262.2 2.9 fusion.146
  265.1 2.9 fusion.144
  268.0 3.8 %fusion.145 = f32[4,128,128]{2,1,0:T(8,128)S(1)} fusion(bf16[4,2048,256]{2,1,0:T(8,128)(2,1)} %bitcast.80, f32[4,128]{1,0:T(4,128)S(1)} %fusion.144, pred[128]{0:T(512)(128)(4,1)S(1)} %get-tuple-element.137, bf16[4,4,128,128]{3,2,1,0:T(8,128)(2,1)S(1)} %get-tuple-element.153, s32[]{:T(128)S(6)} %copy.22), kind=kOutput, calls=%fused_computation.25.clone.1 | convolution fusion | flops 541198848 | bytes 4590596 | tf_op jit(solution)/shard_map/while/body/eval_jaxpr/gqk,gkc->gqc/dot_general | solution.py:57
  271.8 4.5 %fusion.147 = bf16[4,4,128,128]{3,2,1,0:T(8,128)(2,1)} fusion(bf16[4,4,128,128]{3,2,1,0:T(8,128)(2,1)} %get-tuple-element.146, s32[]{:T(128)S(6)} %copy.22, f32[4,128,128]{2,1,0:T(8,128)S(1)} %fusion.145, bf16[4,2048,256]{2,1,0:T(8,128)(2,1)} %bitcast.81, f32[4,128]{1,0:T(4,128)S(1)} %fusion.146, pred[128]{0:T(512)(128)(4,1)S(1)} %get-tuple-element.138, ...), kind=kOutput, calls=%fused_computation.27.clone.1 | convolution fusion | flops 541329920 | bytes 4722688 | tf_op jit(solution)/shard_map/while/body/eval_jaxpr/gqk,gkc->gqc/dot_general | solution.py:57
  276.3 0.7 compare_select_fusion.2
  277.0 0.1 reshape.157
  277.1 8.5 %gather_fusion = bf16[64,128,256]{2,1,0:T(8,128)(2,1)} fusion(bf16[256,128,256]{2,1,0:T(8,128)(2,1)} %get-tuple-element.155, s32[1024]{0:T(1024)S(1)} %pad_clamp_fusion.2), kind=kCustom, calls=%fused_computation.clone.clone.1 | custom fusion | bytes 8388864 | tf_op jit(solution)/shard_map/while/body/eval_jaxpr/gather | solution.py:43
  285.6 2.9 fusion.146
  288.5 2.9 fusion.144
  291.4 3.8 %fusion.145 = f32[4,128,128]{2,1,0:T(8,128)S(1)} fusion(bf16[4,2048,256]{2,1,0:T(8,128)(2,1)} %bitcast.80, f32[4,128]{1,0:T(4,128)S(1)} %fusion.144, pred[128]{0:T(512)(128)(4,1)S(1)} %get-tuple-element.137, bf16[4,4,128,128]{3,2,1,0:T(8,128)(2,1)S(1)} %get-tuple-element.153, s32[]{:T(128)S(6)} %copy.22), kind=kOutput, calls=%fused_computation.25.clone.1 | convolution fusion | flops 541198848 | bytes 4590596 | tf_op jit(solution)/shard_map/while/body/eval_jaxpr/gqk,gkc->gqc/dot_general | solution.py:57
  295.2 4.5 %fusion.147 = bf16[4,4,128,128]{3,2,1,0:T(8,128)(2,1)} fusion(bf16[4,4,128,128]{3,2,1,0:T(8,128)(2,1)} %get-tuple-element.146, s32[]{:T(128)S(6)} %copy.22, f32[4,128,128]{2,1,0:T(8,128)S(1)} %fusion.145, bf16[4,2048,256]{2,1,0:T(8,128)(2,1)} %bitcast.81, f32[4,128]{1,0:T(4,128)S(1)} %fusion.146, pred[128]{0:T(512)(128)(4,1)S(1)} %get-tuple-element.138, ...), kind=kOutput, calls=%fused_computation.27.clone.1 | convolution fusion | flops 541329920 | bytes 4722688 | tf_op jit(solution)/shard_map/while/body/eval_jaxpr/gqk,gkc->gqc/dot_general | solution.py:57
  299.7 0.7 compare_select_fusion.2
  300.4 0.1 reshape.157
  300.5 8.5 %gather_fusion = bf16[64,128,256]{2,1,0:T(8,128)(2,1)} fusion(bf16[256,128,256]{2,1,0:T(8,128)(2,1)} %get-tuple-element.155, s32[1024]{0:T(1024)S(1)} %pad_clamp_fusion.2), kind=kCustom, calls=%fused_computation.clone.clone.1 | custom fusion | bytes 8388864 | tf_op jit(solution)/shard_map/while/body/eval_jaxpr/gather | solution.py:43
  309.0 2.9 fusion.146
  311.9 2.9 fusion.144
  314.8 3.8 %fusion.145 = f32[4,128,128]{2,1,0:T(8,128)S(1)} fusion(bf16[4,2048,256]{2,1,0:T(8,128)(2,1)} %bitcast.80, f32[4,128]{1,0:T(4,128)S(1)} %fusion.144, pred[128]{0:T(512)(128)(4,1)S(1)} %get-tuple-element.137, bf16[4,4,128,128]{3,2,1,0:T(8,128)(2,1)S(1)} %get-tuple-element.153, s32[]{:T(128)S(6)} %copy.22), kind=kOutput, calls=%fused_computation.25.clone.1 | convolution fusion | flops 541198848 | bytes 4590596 | tf_op jit(solution)/shard_map/while/body/eval_jaxpr/gqk,gkc->gqc/dot_general | solution.py:57
  318.6 4.5 %fusion.147 = bf16[4,4,128,128]{3,2,1,0:T(8,128)(2,1)} fusion(bf16[4,4,128,128]{3,2,1,0:T(8,128)(2,1)} %get-tuple-element.146, s32[]{:T(128)S(6)} %copy.22, f32[4,128,128]{2,1,0:T(8,128)S(1)} %fusion.145, bf16[4,2048,256]{2,1,0:T(8,128)(2,1)} %bitcast.81, f32[4,128]{1,0:T(4,128)S(1)} %fusion.146, pred[128]{0:T(512)(128)(4,1)S(1)} %get-tuple-element.138, ...), kind=kOutput, calls=%fused_computation.27.clone.1 | convolution fusion | flops 541329920 | bytes 4722688 | tf_op jit(solution)/shard_map/while/body/eval_jaxpr/gqk,gkc->gqc/dot_general | solution.py:57
  323.0 15.1 %all_to_all.19 = bf16[8,256,128]{2,1,0:T(8,128)(2,1)S(1)} all-to-all(bf16[8,256,128]{2,1,0:T(8,128)(2,1)} %bitcast.88), channel_id=1, replica_groups=mesh['batch'=2,'head'=8,'blk'=16] {'head'}, dimensions={0} | all-to-all | bytes 1048576 | tf_op jit(solution)/shard_map/all_to_all | solution.py:65
  338.1 0.2 copy.15
  338.3 1.5 fusion.114
  (11 shorter events, 0.1 us)
Async XLA Ops:
  6.5 331.8 %copy-start = (bf16[1024,1024]{1,0:T(8,128)(2,1)S(1)}, bf16[1024,1024]{1,0:T(8,128)(2,1)}, u32[]{:S(2)}) copy-start(bf16[1024,1024]{1,0:T(8,128)(2,1)} %param.8) | copy-start | bytes 6291460
  6.5 98.1 %all-gather.6.cloned.1.call-start = ((), (), s32[]{:S(2)}) async-start(), calls=%async_computation.2 | async-start | bytes 4718592 | tf_op jit(solution)/shard_map/all_gather | solution.py:26
  7.3 199.9 %all-gather.4.cloned.1.call-start = ((), (), s32[]{:S(2)}) async-start(), calls=%async_computation.1 | async-start | bytes 17825792 | tf_op jit(solution)/shard_map/all_gather | solution.py:32
  108.7 1.2 copy-start.1
Sparse Core Ops, SparseCore 0:
  9.1 95.4 all-gather.5
  111.0 96.0 all-gather.3
where the time goes:
time: 349 us; the launch traced here: 347 us
  waiting for transfers between devices  189 us (54%)
  local copies, waits for them, and re-layouts  64.1 us (18%)
  matrix products  61.8 us (18%)
  blocking collectives  15.1 us (4%)
  between operations  13.5 us (4%)
    all_gather x1, waiting for transfers between devices, on_device(): source = lax.all_gather(key_value, 'blk', axis=0, tiled=True)  94.9 us
    all_gather x1, waiting for transfers between devices, on_device(): lax.all_gather(own_rows, 'head', axis=0, tiled=True)  93.8 us
    gather x4, local copies, waits for them, and re-layouts, attend(): source_blocks[positions].reshape(group_size, KSEL * BLK, 2 * head_width)  34 us
    dot_general x8, matrix products, attend(): jnp.einsum('gqk,gkc->gqc', weights, value_rows, preferred_element_type=jn...  33 us
    unnamed x7, local copies, waits for them, and re-layouts  25 us
    sub x8, matrix products, attend(): raised = jnp.exp(scores - row_max)  23.2 us
    all_to_all x1, blocking collectives, on_device(): lax.all_to_all(attended, 'head', split_axis=0, concat_axis=1, tiled=True)  15.1 us
  transfers between devices with their start and end apart: 2, of which 2 were waited for; matrix products, arithmetic and copies ran while one was open for 1% of the time, Pallas kernels for 0%

commit v1 on v0

v1 whole, which is shorter than its diff:
```python
import functools

import jax
import jax.numpy as jnp
from jax import lax
from jax.experimental import pallas as pl
from jax.experimental.pallas import tpu as pltpu
from jax.sharding import PartitionSpec as P

D = 1024
H = 16
HD = 64
BLK = 128
KSEL = 16
LSEL = 6
SB = 16
REACH = 8
SUMB = 4
MESH = pl.DeviceIdType.MESH
F32 = jnp.float32
BF16 = jnp.bfloat16


def kernel(
    n_head, n_blk, tok_ref, w_hbm, wo_hbm, pat_ref, out_ref,
    w_v, wo_v, kvs, qs, win, summ, q_v, m_v, l_v, acc_v, attn, ost,
    w_sem, wo_sem, kv_send, kv_recv, q_send, q_recv,
    up_send, up_recv, dn_send, dn_recv, sib_send, sib_recv,
    halo_send, halo_recv, loc_sem, out_send, out_recv,
):
    g = lax.axis_index("head")
    b = lax.axis_index("blk")
    pair = 2 * HD
    half = REACH

    def blk_at(shift):
        return lax.rem(b + n_blk + shift, n_blk)

    sibling = b + 1 - 2 * lax.rem(b, 2)

    def w_copy(k):
        dest = lax.rem(g + k, n_head)
        col = pl.multiple_of(dest * (3 * pair), pair)
        return pltpu.make_async_copy(w_hbm.at[:, pl.ds(col, 3 * pair)], w_v.at[k], w_sem.at[k])

    for k in range(n_head):
        w_copy((k + 1) % n_head).start()
    wo_copy = pltpu.make_async_copy(wo_hbm, wo_v, wo_sem)
    wo_copy.start()

    barrier = pltpu.get_barrier_semaphore()
    for k in range(1, n_head):
        pl.semaphore_signal(
            barrier, inc=1, device_id={"head": lax.rem(g + k, n_head)}, device_id_type=MESH
        )
    for shift in (-2, -1, 1, 2):
        pl.semaphore_signal(
            barrier, inc=1, device_id={"blk": blk_at(shift)}, device_id_type=MESH
        )
    pl.semaphore_wait(barrier, n_head - 1 + 4)

    low = lax.broadcasted_iota(jnp.int32, (1, pair), 1) < HD

    def remote(src, dst, send, recv, **where):
        return pltpu.make_async_remote_copy(
            src_ref=src, dst_ref=dst, send_sem=send, recv_sem=recv,
            device_id=where, device_id_type=MESH,
        )

    def own_win(h):
        return win.at[pl.ds(half + 2 * h, 2)]

    def own_sum(h):
        return summ.at[pl.ds(SUMB * b + 2 * (h - 6), 2)]

    def project(k):
        w_copy(k).wait()
        full = jnp.dot(tok_ref[...], w_v[k], preferred_element_type=F32)
        t0, t1, t2 = full[:, :pair], full[:, pair : 2 * pair], full[:, 2 * pair :]
        queries = pltpu.roll(jnp.where(low, t0, t1), HD, 1).astype(BF16) * BF16(HD**-0.5)
        keys = jnp.where(low, t2, t0).astype(BF16)
        values = jnp.where(low, t1, t2).astype(BF16)
        kvs[k, :, :, :pair] = keys.reshape(2, BLK, pair)
        kvs[k, :, :, pair:] = values.reshape(2, BLK, pair)
        qs[k] = queries.reshape(2, BLK, pair)

    def kv_to(k, dst):
        dest = lax.rem(g + k, n_head)
        return remote(kvs.at[k], dst, kv_send.at[k], kv_recv.at[g], head=dest)

    def q_to(k):
        dest = lax.rem(g + k, n_head)
        return remote(qs.at[k], q_v.at[pl.ds(2 * g, 2)], q_send.at[k], q_recv.at[g], head=dest)

    def first(k, carry):
        project(k)

        @pl.when(g < 6)
        def _():
            kv_to(k, own_win(g)).start()

        @pl.when(g >= 6)
        def _():
            kv_to(k, own_sum(g)).start()

        return carry

    lax.fori_loop(1, n_head, first, 0)
    project(0)

    @pl.when(g < 6)
    def _():
        pltpu.make_async_copy(kvs.at[0], own_win(g), kv_recv.at[g]).start()

    @pl.when(g >= 6)
    def _():
        pltpu.make_async_copy(kvs.at[0], own_sum(g), kv_recv.at[g]).start()

    for k in range(1, n_head):
        q_to(k).start()
    pltpu.make_async_copy(qs.at[0], q_v.at[pl.ds(2 * g, 2)], q_recv.at[g]).start()

    def arrived(ref, sem):
        pltpu.make_async_copy(ref, ref, sem).wait()

    def slot(source, part):
        return summ.at[SUMB * source + part]

    def up_copy(n):
        source = blk_at(-2 * (n // SUMB))
        ref = slot(source, lax.rem(n, SUMB))
        return remote(ref, ref, up_send.at[n], up_recv.at[n], blk=blk_at(2))

    def dn_copy(n):
        source = blk_at(2 * (n // SUMB))
        ref = slot(source, lax.rem(n, SUMB))
        return remote(ref, ref, dn_send.at[n], dn_recv.at[n], blk=blk_at(-2))

    def sib_copy(m, source, part):
        ref = slot(source, part)
        return remote(ref, ref, sib_send.at[m], sib_recv.at[m], blk=sibling)

    def halo_copy(h, src):
        if h < 4:
            return remote(
                src, win.at[pl.ds(3 * half + 2 * h, 2)], halo_send.at[h], halo_recv.at[h],
                blk=blk_at(-1),
            )
        return remote(
            src, win.at[pl.ds(2 * h - half, 2)], halo_send.at[h], halo_recv.at[h], blk=blk_at(1)
        )

    for h in (6, 7):
        arrived(own_sum(h), kv_recv.at[h])
        for part in (2 * (h - 6), 2 * (h - 6) + 1):
            up_copy(part).start()
            dn_copy(part).start()
            sib_copy(part, b, part).start()
        halo_copy(h, own_sum(h)).start()
        pltpu.make_async_copy(own_sum(h), own_win(h), loc_sem.at[h - 6]).start()
    for h in range(6):
        arrived(own_win(h), kv_recv.at[h])
        halo_copy(h, own_win(h)).start()

    n_up = SUMB * (n_blk // 4)
    n_dn = SUMB * (n_blk // 4 - 1)

    def relay(n):
        step, part = n // SUMB + 1, lax.rem(n, SUMB)
        source = blk_at(-2 * step)
        arrived(slot(source, part), up_recv.at[n])

        @pl.when(n < n_up - SUMB)
        def _():
            up_copy(n + SUMB).start()

        sib_copy(SUMB + n, source, part).start()

        @pl.when(n < n_dn)
        def _():
            source = blk_at(2 * step)
            arrived(slot(source, part), dn_recv.at[n])

            @pl.when(n < n_dn - SUMB)
            def _():
                dn_copy(n + SUMB).start()

            sib_copy(SUMB + n_up + n, source, part).start()

    n_pairs = n_head

    def relays(n, carry):
        relay(n)
        return carry

    lax.fori_loop(0, n_up - n_pairs, relays, 0)

    for h in range(n_head):
        arrived(q_v.at[pl.ds(2 * h, 2)], q_recv.at[h])
        if h < 4:
            arrived(win.at[pl.ds(3 * half + 2 * h, 2)], halo_recv.at[h])
        else:
            arrived(win.at[pl.ds(2 * h - half, 2)], halo_recv.at[h])
    for h in (6, 7):
        arrived(own_win(h), loc_sem.at[h - 6])

    def masked_queries(i):
        block = q_v[i]
        zero = jnp.zeros_like(block)
        return jnp.concatenate([jnp.where(low, zero, block), jnp.where(low, block, zero)], axis=0)

    def scores_of(queries, ref, places):
        keys = jnp.concatenate([ref[p, :, :pair] for p in places], axis=0)
        return lax.dot_general(
            queries, keys, (((1,), (1,)), ((), ())), preferred_element_type=F32
        )

    def mixed(weights, ref, places):
        values = jnp.concatenate([ref[p, :, pair:] for p in places], axis=0)
        return jnp.dot(weights.astype(BF16), values, preferred_element_type=F32)

    def window_block(i):
        places = [
            jnp.clip(pat_ref[i, j] - (SB * b - half), 0, SB + 2 * half - 1) for j in range(LSEL)
        ]
        scores = scores_of(masked_queries(i), win, places)
        top = jnp.max(scores, axis=1, keepdims=True)
        raised = jnp.exp(scores - top)
        total = jnp.sum(raised, axis=1, keepdims=True)
        acc_v[i] = mixed(raised, win, places)
        m_v[i] = jnp.broadcast_to(top, (2 * BLK, pair))
        l_v[i] = jnp.broadcast_to(total, (2 * BLK, pair))

    def summary_block(i):
        places = []
        for j in range(LSEL, KSEL):
            block = pat_ref[i, j]
            within = jnp.maximum(lax.rem(block, SB) - (SB - SUMB), 0)
            places.append((block // SB) * SUMB + within)
        scores = scores_of(masked_queries(i), summ, places)
        before = m_v[i]
        top = jnp.maximum(jnp.max(scores, axis=1, keepdims=True), before)
        shrink = jnp.exp(before - top)
        raised = jnp.exp(scores - top[:, :1])
        total = jnp.sum(raised, axis=1, keepdims=True) + l_v[i] * shrink
        product = (mixed(raised, summ, places) + acc_v[i] * shrink) / total
        return jnp.where(low, product[:BLK], product[BLK:]).astype(BF16)

    def window_pair(t, carry):
        window_block(2 * t)
        window_block(2 * t + 1)
        relay(n_up - n_pairs + t)
        return carry

    lax.fori_loop(0, n_pairs, window_pair, 0)

    other = sibling
    for m in range(SUMB):
        arrived(slot(other, m), sib_recv.at[m])

    def others(n, carry):
        step, part = n // SUMB + 1, lax.rem(n, SUMB)
        arrived(slot(lax.rem(other + n_blk - 2 * step, n_blk), part), sib_recv.at[SUMB + n])

        @pl.when(n < n_dn)
        def _():
            arrived(slot(lax.rem(other + 2 * step, n_blk), part), sib_recv.at[SUMB + n_up + n])

        return carry

    lax.fori_loop(0, n_up, others, 0)

    columns = pl.ds(pl.multiple_of(g * pair, pair), pair)

    def out_to(t):
        dest = lax.rem(g + 1 + t, n_head)
        return remote(ost.at[t], attn.at[:, columns], out_send.at[t], out_recv.at[g], head=dest)

    def summary_pair(t, carry):
        dest = lax.rem(g + 1 + t, n_head)
        ost[t, :BLK] = summary_block(2 * dest)
        ost[t, BLK:] = summary_block(2 * dest + 1)

        @pl.when(t < n_head - 1)
        def _():
            out_to(t).start()

        return carry

    lax.fori_loop(0, n_pairs, summary_pair, 0)
    pltpu.make_async_copy(ost.at[n_head - 1], attn.at[:, columns], out_recv.at[g]).start()

    wo_copy.wait()
    for h in range(n_head):
        arrived(attn.at[:, pl.ds(h * pair, pair)], out_recv.at[h])
    out_ref[...] = jnp.dot(attn[...], wo_v[...], preferred_element_type=F32).astype(BF16)

    for k in range(1, n_head):
        kv_to(k, own_win(0)).wait_send()
        q_to(k).wait_send()
        out_to(k - 1).wait_send()
    for h in range(n_head):
        halo_copy(h, own_win(h)).wait_send()

    def sent(n, carry):
        up_copy(n).wait_send()
        sib_copy(n, b, 0).wait_send()
        sib_copy(n_up + n, b, 0).wait_send()

        @pl.when(n < n_dn)
        def _():
            dn_copy(n).wait_send()

        return carry

    lax.fori_loop(0, n_up, sent, 0)


def on_device(n_head, n_blk, tokens, proj_weight, out_weight, pattern):
    rows = tokens.shape[1]
    pair = 2 * HD
    n_query = pattern.shape[0]
    n_up = SUMB * (n_blk // 4)
    n_dn = n_up - SUMB
    n_sib = SUMB * (n_blk // 2)
    dma = pltpu.SemaphoreType.DMA
    out = pl.pallas_call(
        functools.partial(kernel, n_head, n_blk),
        out_shape=jax.ShapeDtypeStruct((rows, D), BF16),
        in_specs=[
            pl.BlockSpec(memory_space=pltpu.VMEM),
            pl.BlockSpec(memory_space=pl.ANY),
            pl.BlockSpec(memory_space=pl.ANY),
            pl.BlockSpec(memory_space=pltpu.SMEM),
        ],
        out_specs=pl.BlockSpec(memory_space=pltpu.VMEM),
        scratch_shapes=[
            pltpu.VMEM((n_head, D, 3 * pair), BF16),
            pltpu.VMEM((D, D), BF16),
            pltpu.VMEM((n_head, 2, BLK, 2 * pair), BF16),
            pltpu.VMEM((n_head, 2, BLK, pair), BF16),
            pltpu.VMEM((SB + 2 * REACH, BLK, 2 * pair), BF16),
            pltpu.VMEM((SUMB * n_blk, BLK, 2 * pair), BF16),
            pltpu.VMEM((n_query, BLK, pair), BF16),
            pltpu.VMEM((n_query, 2 * BLK, pair), F32),
            pltpu.VMEM((n_query, 2 * BLK, pair), F32),
            pltpu.VMEM((n_query, 2 * BLK, pair), F32),
            pltpu.VMEM((rows, D), BF16),
            pltpu.VMEM((n_head, rows, pair), BF16),
            dma((n_head,)),
            dma,
            dma((n_head,)),
            dma((n_head,)),
            dma((n_head,)),
            dma((n_head,)),
            dma((n_up,)),
            dma((n_up,)),
            dma((n_dn,)),
            dma((n_dn,)),
            dma((n_sib,)),
            dma((n_sib,)),
            dma((n_head,)),
            dma((n_head,)),
            dma((2,)),
            dma((n_head,)),
            dma((n_head,)),
        ],
        compiler_params=pltpu.CompilerParams(
            collective_id=0, has_side_effects=True, vmem_limit_bytes=48 * 1024 * 1024
        ),
    )(tokens[0], proj_weight, out_weight, pattern)
    return out.reshape(1, rows, D)


def solution(mesh):
    return jax.shard_map(
        functools.partial(on_device, mesh.shape["head"], mesh.shape["blk"]),
        mesh=mesh,
        in_specs=(P(("batch", "blk"), "head", None), P(), P(), P(("batch", "blk"), None)),
        out_specs=P(("batch", "blk"), "head", None),
        check_vma=False,
    )
```

time: 349 us -> 77 us (0.22)
  the two profiles are of different devices: /device:TPU:6 before, /device:TPU:11 now
where the time goes in v1:
time: 77 us; the launch traced here: 76.8 us
  Pallas kernels  72.6 us (94%)
  local copies, waits for them, and re-layouts  4.12 us (5%)
    pallas_call x1, Pallas kernels, on_device(): pl.pallas_call(functools.partial(kernel, n_head, n_blk), out_shape=jax.Sh...  72.6 us
    unnamed x7, local copies, waits for them, and re-layouts  4.12 us

profile of v1, /device:TPU:11, one launch (start us, length us, event | category | flops | bytes accessed | tf_op | source)
XLA Modules:
  0.0 76.8 jit_solution(12540368812187560800)
XLA Ops:
  0.0 0.0 copy-start
  0.0 1.6 %copy-done = bf16[1024,1024]{1,0:T(8,128)(2,1)S(1)} copy-done((bf16[1024,1024]{1,0:T(8,128)(2,1)S(1)}, bf16[1024,1024]{1,0:T(8,128)(2,1)}, u32[]{:S(2)}) %copy-start) | copy-done | bytes 2097176
  1.6 0.0 copy-start.1
  1.6 1.0 %copy-done.1 = bf16[1,256,1024]{2,1,0:T(8,128)(2,1)S(1)} copy-done((bf16[1,256,1024]{2,1,0:T(8,128)(2,1)S(1)}, bf16[1,256,1024]{2,1,0:T(8,128)(2,1)}, u32[]{:S(2)}) %copy-start.1) | copy-done | bytes 524312
  2.6 0.0 copy-start.2
  2.6 0.7 copy-done.2
  3.3 72.6 %shard_map.46 = bf16[256,1024]{1,0:T(8,128)(2,1)S(1)} custom-call(bf16[256,1024]{1,0:T(8,128)(2,1)S(1)} %bitcast.3, bf16[1024,3072]{1,0:T(8,128)(2,1)} %w_hbm.1, bf16[1024,1024]{1,0:T(8,128)(2,1)S(1)} %copy-done, s32[16,16]{1,0:T(8,128)S(1)} %copy-done.2), custom_call_target="tpu_custom_call" | custom-call | tf_op jit(solution)/shard_map/pallas_call | solution.py:327
  76.0 0.8 %copy.6 = bf16[1,256,1024]{2,1,0:T(8,128)(2,1)} copy(bf16[1,256,1024]{2,1,0:T(8,128)(2,1)S(1)} %bitcast.2) | data formatting | bytes 1048576
Async XLA Ops:
  0.0 1.6 %copy-start = (bf16[1024,1024]{1,0:T(8,128)(2,1)S(1)}, bf16[1024,1024]{1,0:T(8,128)(2,1)}, u32[]{:S(2)}) copy-start(bf16[1024,1024]{1,0:T(8,128)(2,1)} %wo_hbm.1) | copy-start | bytes 6291460
  1.6 1.0 %copy-start.1 = (bf16[1,256,1024]{2,1,0:T(8,128)(2,1)S(1)}, bf16[1,256,1024]{2,1,0:T(8,128)(2,1)}, u32[]{:S(2)}) copy-start(bf16[1,256,1024]{2,1,0:T(8,128)(2,1)} %param.4) | copy-start | bytes 1572868
  2.6 0.7 copy-start.2

commit v2 on v0

v2 whole, which is shorter than its diff:
```python
import functools

import jax
import jax.numpy as jnp
from jax import lax
from jax.experimental import pallas as pl
from jax.experimental.pallas import tpu as pltpu
from jax.sharding import PartitionSpec as P

D = 1024
H = 16
HD = 64
BLK = 128
KSEL = 16
LSEL = 6
SSEL = 10
SB = 16
REACH = 8
SUMB = 4
MESH = pl.DeviceIdType.MESH
F32 = jnp.float32
BF16 = jnp.bfloat16
PAIR = 2 * HD
FIRST_SUM = (SB - SUMB) // 2


def kernel(
    n_head, n_blk, tok_hbm, w_hbm, wo_hbm, pat_hbm, out_ref,
    tok_v, w_v, wo_v, pat_ref, ks, vs, qs, win_k, win_v, sum_k, sum_v,
    q_v, ml_v, p_v, a_v, c_v, attn, ost,
    in_sem, w_sem, k_send, k_recv, v_send, v_recv, q_send, q_recv,
    up_send, up_recv, dn_send, dn_recv, sib_send, sib_recv,
    halo_send, halo_recv, loc_sem, out_send, out_recv,
):
    g = lax.axis_index("head")
    b = lax.axis_index("blk")
    core = lax.rem(b, 2)
    sibling = b + 1 - 2 * core
    half = REACH
    chunks = SUMB // 2
    summary_owner = g >= FIRST_SUM
    ks_kinds = (sum_k, sum_v)
    steps = n_blk // 4
    n_up = (chunks * steps, chunks * steps - 1)
    n_dn = (chunks * (steps - 1), chunks * (steps - 1) + 1)

    def shifted(position, shift):
        return lax.rem(position + n_blk + shift, n_blk)

    def w_copy(k):
        dest = lax.rem(g + k, n_head)
        col = pl.multiple_of(dest * (3 * PAIR), PAIR)
        return pltpu.make_async_copy(w_hbm.at[:, pl.ds(col, 3 * PAIR)], w_v.at[k], w_sem.at[k])

    tok_copy = pltpu.make_async_copy(tok_hbm, tok_v, in_sem.at[0])
    wo_copy = pltpu.make_async_copy(wo_hbm, wo_v, in_sem.at[1])
    pat_copy = pltpu.make_async_copy(pat_hbm, pat_ref, in_sem.at[2])
    tok_copy.start()
    for k in range(n_head):
        w_copy((k + 1) % n_head).start()
    pat_copy.start()
    wo_copy.start()

    barrier = pltpu.get_barrier_semaphore()
    for k in range(1, n_head):
        pl.semaphore_signal(
            barrier, inc=1, device_id={"head": lax.rem(g + k, n_head)}, device_id_type=MESH
        )
    for shift in (-2, -1, 1, 2):
        pl.semaphore_signal(
            barrier, inc=1, device_id={"blk": shifted(b, shift)}, device_id_type=MESH
        )

    low = lax.broadcasted_iota(jnp.int32, (1, PAIR), 1) < HD

    def remote(src, dst, send, recv, **where):
        return pltpu.make_async_remote_copy(
            src_ref=src, dst_ref=dst, send_sem=send, recv_sem=recv,
            device_id=where, device_id_type=MESH,
        )

    def arrived(ref, sem):
        pltpu.make_async_copy(ref, ref, sem).wait()

    def own_win(ref, h):
        return ref.at[pl.ds(half + 2 * h, 2)]

    def own_sum(ref, h):
        return ref.at[pl.ds(SUMB * b + 2 * (h - FIRST_SUM), 2)]

    def project(k, carry):
        w_copy(k).wait()
        full = jnp.dot(tok_v[...], w_v[k], preferred_element_type=F32)
        t0, t1, t2 = full[:, :PAIR], full[:, PAIR : 2 * PAIR], full[:, 2 * PAIR :]
        queries = pltpu.roll(jnp.where(low, t0, t1), HD, 1).astype(BF16) * BF16(HD**-0.5)
        ks[k] = jnp.where(low, t2, t0).astype(BF16).reshape(2, BLK, PAIR)
        vs[k] = jnp.where(low, t1, t2).astype(BF16).reshape(2, BLK, PAIR)
        qs[k] = queries.reshape(2, BLK, PAIR)
        return carry

    tok_copy.wait()
    lax.fori_loop(1, n_head, project, 0)
    project(0, 0)
    pl.semaphore_wait(barrier, n_head - 1 + 4)

    def exchange(stage, send, recv, k, dst):
        return remote(stage.at[k], dst, send.at[k], recv.at[g], head=lax.rem(g + k, n_head))

    def send_all(stage, send, recv, dst):
        for k in range(1, n_head):
            exchange(stage, send, recv, k, dst).start()
        pltpu.make_async_copy(stage.at[0], dst, recv.at[g]).start()

    own_q = q_v.at[pl.ds(2 * g, 2)]

    @pl.when(summary_owner)
    def _():
        send_all(ks, k_send, k_recv, own_sum(sum_k, g))

    send_all(qs, q_send, q_recv, own_q)

    @pl.when(summary_owner)
    def _():
        send_all(vs, v_send, v_recv, own_sum(sum_v, g))

    def piece(kind, source, part):
        return ks_kinds[kind].at[pl.ds(SUMB * source + 2 * part, 2)]

    def dn_part(kind, n):
        part = lax.rem(n, chunks)
        return part if kind == 0 else chunks - 1 - part

    def up_copy(kind, n):
        ref = piece(kind, shifted(b, -2 * (n // chunks)), lax.rem(n, chunks))
        return remote(
            ref, ref, up_send.at[kind, n], up_recv.at[kind, n], blk=shifted(b, 2)
        )

    def dn_copy(kind, n):
        ref = piece(kind, shifted(b, 2 * (n // chunks)), dn_part(kind, n))
        return remote(
            ref, ref, dn_send.at[kind, n], dn_recv.at[kind, n], blk=shifted(b, -2)
        )

    def sib_copy(kind, m, ref):
        return remote(ref, ref, sib_send.at[kind, m], sib_recv.at[kind, m], blk=sibling)

    def start_own(kind):
        for part in range(chunks):
            ref = piece(kind, b, part)
            h = FIRST_SUM + part
            arrived(ref, (k_recv, v_recv)[kind].at[h])
            up_copy(kind, part).start()
            dn_copy(kind, part if kind == 0 else chunks - 1 - part).start()
            sib_copy(kind, part, ref).start()
            pltpu.make_async_copy(
                ref, own_win((win_k, win_v)[kind], h), loc_sem.at[kind, part]
            ).start()

    def relay(kind, n):
        ref = piece(kind, shifted(b, -2 * (n // chunks + 1)), lax.rem(n, chunks))
        arrived(ref, up_recv.at[kind, n])

        @pl.when(n < n_up[kind] - chunks)
        def _():
            up_copy(kind, n + chunks).start()

        sib_copy(kind, chunks + n, ref).start()

        @pl.when(n < n_dn[kind])
        def _():
            back = piece(kind, shifted(b, 2 * (n // chunks + 1)), dn_part(kind, n))
            arrived(back, dn_recv.at[kind, n])

            @pl.when(n < n_dn[kind] - chunks)
            def _():
                dn_copy(kind, n + chunks).start()

            sib_copy(kind, chunks + n_up[kind] + n, back).start()

    start_own(0)

    @pl.when(jnp.logical_not(summary_owner))
    def _():
        send_all(ks, k_send, k_recv, own_win(win_k, g))
        send_all(vs, v_send, v_recv, own_win(win_v, g))

    def relays(n, carry):
        relay(0, n)
        return carry

    lax.fori_loop(0, n_up[0] - chunks, relays, 0)
    start_own(1)
    lax.fori_loop(n_up[0] - chunks, n_up[0], relays, 0)

    early = chunks * (1 - core)

    def other_arrived(kind, m):
        s = sibling
        if kind == 0:
            down_part = lambda n: lax.rem(n, chunks)
        else:
            down_part = lambda n: chunks - 1 - lax.rem(n, chunks)

        @pl.when(m < chunks)
        def _():
            arrived(piece(kind, s, m), sib_recv.at[kind, m])

        n = m - chunks

        @pl.when(jnp.logical_and(n >= 0, n < n_up[kind]))
        def _():
            arrived(
                piece(kind, shifted(s, -2 * (n // chunks + 1)), lax.rem(n, chunks)),
                sib_recv.at[kind, m],
            )

        n2 = n - n_up[kind]

        @pl.when(n2 >= 0)
        def _():
            arrived(
                piece(kind, shifted(s, 2 * (n2 // chunks + 1)), down_part(n2)),
                sib_recv.at[kind, m],
            )

    def copy_below(kind):
        for part in range(chunks):
            other_arrived(kind, early + part)
            pltpu.make_async_copy(
                piece(kind, shifted(b, -1), part),
                (win_k, win_v)[kind].at[pl.ds(SUMB + 2 * part, 2)],
                loc_sem.at[kind, chunks + part],
            ).start()

    def others(kind):
        def body(m, carry):
            @pl.when(jnp.logical_or(m < early, m >= early + chunks))
            def _():
                other_arrived(kind, m)

            return carry

        lax.fori_loop(0, chunks * n_blk // 2, body, 0)

    def halo_place(ref, h):
        start = 3 * half + 2 * h if 2 * h < half else 2 * h - half
        return ref.at[pl.ds(start, 2)]

    def halo_copy(kind, h):
        ref = (win_k, win_v)[kind]
        shift = -1 if 2 * h < half else 1
        return remote(
            own_win(ref, h), halo_place(ref, h), halo_send.at[kind, h], halo_recv.at[kind, h],
            blk=shifted(b, shift),
        )

    copy_below(0)
    others(0)
    for h in range(n_head):
        arrived(q_v.at[pl.ds(2 * h, 2)], q_recv.at[h])
    pat_copy.wait()

    def masked_queries(i):
        block = q_v[i]
        zero = jnp.zeros_like(block)
        return jnp.concatenate([jnp.where(low, zero, block), jnp.where(low, block, zero)], axis=0)

    def scores_of(queries, ref, places):
        keys = jnp.concatenate([ref[p] for p in places], axis=0)
        return lax.dot_general(
            queries, keys, (((1,), (1,)), ((), ())), preferred_element_type=F32
        )

    def mixed(weights, ref, places):
        values = jnp.concatenate([ref[p] for p in places], axis=0)
        return jnp.dot(weights, values, preferred_element_type=F32)

    def by_head(rows):
        return jnp.where(low, rows[:BLK], rows[BLK:])

    def summary_places(i):
        places = []
        for j in range(LSEL, KSEL):
            block = pat_ref[i, j]
            within = jnp.maximum(lax.rem(block, SB) - (SB - SUMB), 0)
            places.append((block // SB) * SUMB + within)
        return places

    def summary_weights(i):
        scores = scores_of(masked_queries(i), sum_k, summary_places(i))
        top = jnp.max(scores, axis=1, keepdims=True)
        raised = jnp.exp(scores - top)
        p_v[i] = raised.astype(BF16)
        total = jnp.sum(raised, axis=1, keepdims=True)
        ml_v[i] = jnp.where(low, top, total)

    def window_block(i):
        places = [
            jnp.clip(pat_ref[i, j] - (SB * b - half), 0, SB + 2 * half - 1) for j in range(LSEL)
        ]
        scores = scores_of(masked_queries(i), win_k, places)
        kept = ml_v[i]
        far_top, far_total = kept[:, :1], kept[:, HD : HD + 1]
        top = jnp.maximum(jnp.max(scores, axis=1, keepdims=True), far_top)
        raised = jnp.exp(scores - top)
        shrink = jnp.exp(far_top - top)
        inverse = 1.0 / (jnp.sum(raised, axis=1, keepdims=True) + far_total * shrink)
        a_v[i] = by_head(mixed(raised.astype(BF16), win_v, places) * inverse)
        c_v[i] = by_head(jnp.broadcast_to(shrink * inverse, (2 * BLK, PAIR)))

    def finish_block(i):
        product = mixed(p_v[i], sum_v, summary_places(i))
        return (a_v[i] + c_v[i] * by_head(product)).astype(BF16)

    def weights_pair(t, carry):
        summary_weights(2 * t)
        summary_weights(2 * t + 1)

        @pl.when(t < n_up[1])
        def _():
            relay(1, t)

        @pl.when(t == 2)
        def _():
            for h in range(FIRST_SUM):
                for kind in range(2):
                    arrived(own_win((win_k, win_v)[kind], h), (k_recv, v_recv)[kind].at[h])
                    halo_copy(kind, h).start()

        return carry

    lax.fori_loop(0, n_head, weights_pair, 0)

    copy_below(1)
    for kind in range(2):
        ref = (win_k, win_v)[kind]
        for h in range(FIRST_SUM):
            arrived(halo_place(ref, h), halo_recv.at[kind, h])
        for part in range(chunks):
            arrived(own_win(ref, FIRST_SUM + part), loc_sem.at[kind, part])
            arrived(ref.at[pl.ds(SUMB + 2 * part, 2)], loc_sem.at[kind, chunks + part])

    def window_pair(t, carry):
        window_block(2 * t)
        window_block(2 * t + 1)
        return carry

    lax.fori_loop(0, n_head, window_pair, 0)
    others(1)

    columns = pl.ds(pl.multiple_of(g * PAIR, PAIR), PAIR)

    def out_to(t):
        dest = lax.rem(g + 1 + t, n_head)
        return remote(ost.at[t], attn.at[:, columns], out_send.at[t], out_recv.at[g], head=dest)

    def finish_pair(t, carry):
        dest = lax.rem(g + 1 + t, n_head)
        ost[t, :BLK] = finish_block(2 * dest)
        ost[t, BLK:] = finish_block(2 * dest + 1)

        @pl.when(t < n_head - 1)
        def _():
            out_to(t).start()

        return carry

    lax.fori_loop(0, n_head, finish_pair, 0)
    pltpu.make_async_copy(ost.at[n_head - 1], attn.at[:, columns], out_recv.at[g]).start()

    wo_copy.wait()
    for h in range(n_head):
        arrived(attn.at[:, pl.ds(h * PAIR, PAIR)], out_recv.at[h])
    out_ref[...] = jnp.dot(attn[...], wo_v[...], preferred_element_type=F32).astype(BF16)

    for k in range(1, n_head):
        exchange(ks, k_send, k_recv, k, own_q).wait_send()
        exchange(vs, v_send, v_recv, k, own_q).wait_send()
        exchange(qs, q_send, q_recv, k, own_q).wait_send()
        out_to(k - 1).wait_send()
    for kind in range(2):
        for h in range(FIRST_SUM):
            halo_copy(kind, h).wait_send()

        def sent(m, carry, kind=kind):
            sib_copy(kind, m, piece(kind, b, 0)).wait_send()

            @pl.when(m < n_up[kind])
            def _():
                up_copy(kind, m).wait_send()

            @pl.when(m < n_dn[kind])
            def _():
                dn_copy(kind, m).wait_send()

            return carry

        lax.fori_loop(0, chunks * n_blk // 2, sent, 0)


def on_device(n_head, n_blk, tokens, proj_weight, out_weight, pattern):
    rows = tokens.shape[1]
    n_query = pattern.shape[0]
    n_hop = SUMB * (n_blk // 8)
    n_sib = SUMB * (n_blk // 4)
    dma = pltpu.SemaphoreType.DMA
    blocks = lambda *lead: pltpu.VMEM((*lead, BLK, PAIR), BF16)
    out = pl.pallas_call(
        functools.partial(kernel, n_head, n_blk),
        out_shape=jax.ShapeDtypeStruct((rows, D), BF16),
        in_specs=[pl.BlockSpec(memory_space=pl.ANY)] * 4,
        out_specs=pl.BlockSpec(memory_space=pltpu.VMEM),
        scratch_shapes=[
            pltpu.VMEM((rows, D), BF16),
            pltpu.VMEM((n_head, D, 3 * PAIR), BF16),
            pltpu.VMEM((D, D), BF16),
            pltpu.SMEM((n_query, KSEL), jnp.int32),
            blocks(n_head, 2),
            blocks(n_head, 2),
            blocks(n_head, 2),
            blocks(SB + 2 * REACH),
            blocks(SB + 2 * REACH),
            blocks(SUMB * n_blk),
            blocks(SUMB * n_blk),
            blocks(n_query),
            pltpu.VMEM((n_query, 2 * BLK, PAIR), F32),
            pltpu.VMEM((n_query, 2 * BLK, SSEL * BLK), BF16),
            pltpu.VMEM((n_query, BLK, PAIR), F32),
            pltpu.VMEM((n_query, BLK, PAIR), F32),
            pltpu.VMEM((rows, D), BF16),
            pltpu.VMEM((n_head, rows, PAIR), BF16),
            dma((3,)),
            dma((n_head,)),
            dma((n_head,)),
            dma((n_head,)),
            dma((n_head,)),
            dma((n_head,)),
            dma((n_head,)),
            dma((n_head,)),
            dma((2, n_hop)),
            dma((2, n_hop)),
            dma((2, n_hop)),
            dma((2, n_hop)),
            dma((2, n_sib)),
            dma((2, n_sib)),
            dma((2, FIRST_SUM)),
            dma((2, FIRST_SUM)),
            dma((2, SUMB)),
            dma((n_head,)),
            dma((n_head,)),
        ],
        compiler_params=pltpu.CompilerParams(
            collective_id=0, has_side_effects=True, vmem_limit_bytes=56 * 1024 * 1024
        ),
    )(tokens[0], proj_weight, out_weight, pattern)
    return out.reshape(1, rows, D)


def solution(mesh):
    return jax.shard_map(
        functools.partial(on_device, mesh.shape["head"], mesh.shape["blk"]),
        mesh=mesh,
        in_specs=(P(("batch", "blk"), "head", None), P(), P(), P(("batch", "blk"), None)),
        out_specs=P(("batch", "blk"), "head", None),
        check_vma=False,
    )
```

time: 349 us -> 79.4 us (0.23)
  waiting for transfers between devices: 189 us -> 0 us
  Pallas kernels: 0 us -> 77.4 us
  local copies, waits for them, and re-layouts: 64.1 us -> 1.87 us
  matrix products: 61.8 us -> 0 us
  blocking collectives: 15.1 us -> 0 us
  between operations: 13.5 us -> 0.01 us
    all_gather x2 -> x0, waiting for transfers between devices: 189 us -> none  [the longest x1 94.9 us: on_device(): source = lax.all_gather(key_value, 'blk', axis=0, tiled=True)]
    pallas_call x0 -> x1, Pallas kernels: none -> 77.4 us  [on_device(): pl.pallas_call(functools.partial(kernel, n_head, n_blk), out_shape=jax.Sh...]
    dot_general x10 -> x0, matrix products: 38.6 us -> none  [the longest x8 33 us: attend(): jnp.einsum('gqk,gkc->gqc', weights, value_rows, preferred_element_type=jn...]
    gather x4 -> x0, local copies, waits for them, and re-layouts: 34 us -> none  [attend(): source_blocks[positions].reshape(group_size, KSEL * BLK, 2 * head_width)]
    sub x8 -> x0, matrix products: 23.2 us -> none  [attend(): raised = jnp.exp(scores - row_max)]
    unnamed x7 -> x1, local copies, waits for them, and re-layouts: 25 us -> 1.87 us
    all_to_all x1 -> x0, blocking collectives: 15.1 us -> none  [on_device(): lax.all_to_all(attended, 'head', split_axis=0, concat_axis=1, tiled=True)]
  transfers between devices with their start and end apart: 2 -> 0, of which waited for: 2 -> 0; matrix products, arithmetic and copies ran while one was open for 1% -> 0% of each run, Pallas kernels for 0% -> 0%
where the time goes in v2:
time: 79.4 us; the launch traced here: 79.3 us
  Pallas kernels  77.4 us (97%)
  local copies, waits for them, and re-layouts  1.87 us (2%)
    pallas_call x1, Pallas kernels, on_device(): pl.pallas_call(functools.partial(kernel, n_head, n_blk), out_shape=jax.Sh...  77.4 us
    unnamed x1, local copies, waits for them, and re-layouts  1.87 us

profile of v2, /device:TPU:6, one launch (start us, length us, event | category | flops | bytes accessed | tf_op | source)
XLA Modules:
  0.0 79.3 jit_solution(16408883533644090584)
XLA Ops:
  0.0 77.4 %shard_map.46 = bf16[256,1024]{1,0:T(8,128)(2,1)} custom-call(bf16[256,1024]{1,0:T(8,128)(2,1)} %bitcast.3, bf16[1024,3072]{1,0:T(8,128)(2,1)} %w_hbm.1, bf16[1024,1024]{1,0:T(8,128)(2,1)} %wo_hbm.1, s32[16,16]{1,0:T(8,128)} %pat_hbm.1), custom_call_target="tpu_custom_call" | custom-call | tf_op jit(solution)/shard_map/pallas_call | solution.py:409
  77.4 1.9 %copy.6 = bf16[1,256,1024]{2,1,0:T(8,128)(2,1)} copy(bf16[1,256,1024]{2,1,0:T(8,128)(2,1)} %bitcast.2) | data formatting | bytes 1048576

commit v3 on v2

--- a/solution.py
+++ b/solution.py
@@ -27,7 +27,7 @@
 def kernel(
     n_head, n_blk, tok_hbm, w_hbm, wo_hbm, pat_hbm, out_ref,
     tok_v, w_v, wo_v, pat_ref, ks, vs, qs, win_k, win_v, sum_k, sum_v,
-    q_v, ml_v, p_v, a_v, c_v, attn, ost,
+    q_v, m_v, p_v, near_v, near_m, s_a, s_b, attn, ost,
     in_sem, w_sem, k_send, k_recv, v_send, v_recv, q_send, q_recv,
     up_send, up_recv, dn_send, dn_recv, sib_send, sib_recv,
     halo_send, halo_recv, loc_sem, out_send, out_recv,
@@ -94,34 +94,49 @@
         t0, t1, t2 = full[:, :PAIR], full[:, PAIR : 2 * PAIR], full[:, 2 * PAIR :]
         queries = pltpu.roll(jnp.where(low, t0, t1), HD, 1).astype(BF16) * BF16(HD**-0.5)
         ks[k] = jnp.where(low, t2, t0).astype(BF16).reshape(2, BLK, PAIR)
-        vs[k] = jnp.where(low, t1, t2).astype(BF16).reshape(2, BLK, PAIR)
+        values = jnp.where(low, t1, t2)
+        for half_block in range(2):
+            vs[k, half_block] = values[half_block * BLK : (half_block + 1) * BLK].T.astype(BF16)
         qs[k] = queries.reshape(2, BLK, PAIR)
         return carry
 
-    tok_copy.wait()
-    lax.fori_loop(1, n_head, project, 0)
-    project(0, 0)
-    pl.semaphore_wait(barrier, n_head - 1 + 4)
-
     def exchange(stage, send, recv, k, dst):
         return remote(stage.at[k], dst, send.at[k], recv.at[g], head=lax.rem(g + k, n_head))
+
+    own_q = q_v.at[pl.ds(2 * g, 2)]
 
     def send_all(stage, send, recv, dst):
         for k in range(1, n_head):
             exchange(stage, send, recv, k, dst).start()
         pltpu.make_async_copy(stage.at[0], dst, recv.at[g]).start()
 
-    own_q = q_v.at[pl.ds(2 * g, 2)]
+    def send_far_keys(k):
+        @pl.when(summary_owner)
+        def _():
+            exchange(ks, k_send, k_recv, k, own_sum(sum_k, g)).start()
+
+    def project_and_send(k, carry):
+        project(k, carry)
+        send_far_keys(k)
+        return carry
+
+    tok_copy.wait()
+    early_groups = 3
+    lax.fori_loop(1, 1 + early_groups, project, 0)
+    pl.semaphore_wait(barrier, n_head - 1 + 4)
+    for k in range(1, 1 + early_groups):
+        send_far_keys(k)
+    lax.fori_loop(1 + early_groups, n_head, project_and_send, 0)
+    project(0, 0)
 
     @pl.when(summary_owner)
     def _():
-        send_all(ks, k_send, k_recv, own_sum(sum_k, g))
-
-    send_all(qs, q_send, q_recv, own_q)
-
-    @pl.when(summary_owner)
+        pltpu.make_async_copy(ks.at[0], own_sum(sum_k, g), k_recv.at[g]).start()
+        send_all(vs, v_send, v_recv, own_sum(sum_v, g))
+
+    @pl.when(jnp.logical_not(summary_owner))
     def _():
-        send_all(vs, v_send, v_recv, own_sum(sum_v, g))
+        send_all(qs, q_send, q_recv, own_q)
 
     def piece(kind, source, part):
         return ks_kinds[kind].at[pl.ds(SUMB * source + 2 * part, 2)]
@@ -185,13 +200,20 @@
         send_all(ks, k_send, k_recv, own_win(win_k, g))
         send_all(vs, v_send, v_recv, own_win(win_v, g))
 
+    for n in range(chunks):
+        relay(0, n)
+    start_own(1)
+
+    @pl.when(summary_owner)
+    def _():
+        send_all(qs, q_send, q_recv, own_q)
+
     def relays(n, carry):
         relay(0, n)
+        relay(1, n - chunks)
         return carry
 
-    lax.fori_loop(0, n_up[0] - chunks, relays, 0)
-    start_own(1)
-    lax.fori_loop(n_up[0] - chunks, n_up[0], relays, 0)
+    lax.fori_loop(chunks, 2 * chunks, relays, 0)
 
     early = chunks * (1 - core)
 
@@ -255,8 +277,13 @@
             blk=shifted(b, shift),
         )
 
-    copy_below(0)
-    others(0)
+    for h in range(FIRST_SUM):
+        for kind in range(2):
+            arrived(own_win((win_k, win_v)[kind], h), (k_recv, v_recv)[kind].at[h])
+            halo_copy(kind, h).start()
+    lax.fori_loop(2 * chunks, n_up[0] - chunks, relays, 0)
+    for kind in range(2):
+        copy_below(kind)
     for h in range(n_head):
         arrived(q_v.at[pl.ds(2 * h, 2)], q_recv.at[h])
     pat_copy.wait()
@@ -266,18 +293,23 @@
         zero = jnp.zeros_like(block)
         return jnp.concatenate([jnp.where(low, zero, block), jnp.where(low, block, zero)], axis=0)
 
-    def scores_of(queries, ref, places):
+    def scores_of(i, ref, places):
         keys = jnp.concatenate([ref[p] for p in places], axis=0)
         return lax.dot_general(
-            queries, keys, (((1,), (1,)), ((), ())), preferred_element_type=F32
-        )
+            keys, masked_queries(i), (((1,), (1,)), ((), ())), preferred_element_type=F32
+        )
+
+    ones = jnp.ones((16, BLK), BF16)
 
     def mixed(weights, ref, places):
-        values = jnp.concatenate([ref[p] for p in places], axis=0)
-        return jnp.dot(weights, values, preferred_element_type=F32)
-
-    def by_head(rows):
-        return jnp.where(low, rows[:BLK], rows[BLK:])
+        values = jnp.concatenate(
+            [jnp.concatenate([ref[p], ones], axis=0) for p in places], axis=1
+        )
+        product = jnp.dot(values, weights, preferred_element_type=F32)
+        return (
+            (product[:HD, :BLK], product[HD:PAIR, BLK:]),
+            product[PAIR : PAIR + 1],
+        )
 
     def summary_places(i):
         places = []
@@ -287,52 +319,46 @@
             places.append((block // SB) * SUMB + within)
         return places
 
-    def summary_weights(i):
-        scores = scores_of(masked_queries(i), sum_k, summary_places(i))
-        top = jnp.max(scores, axis=1, keepdims=True)
-        raised = jnp.exp(scores - top)
-        p_v[i] = raised.astype(BF16)
-        total = jnp.sum(raised, axis=1, keepdims=True)
-        ml_v[i] = jnp.where(low, top, total)
-
-    def window_block(i):
-        places = [
+    def summary_scores(i, buffer):
+        scores = scores_of(i, sum_k, summary_places(i))
+        buffer[...] = scores
+        m_v[i] = jnp.broadcast_to(jnp.max(scores, axis=0, keepdims=True), (8, 2 * BLK))
+
+    def summary_raise(i, buffer, top):
+        p_v[i] = jnp.exp(buffer[...] - top).astype(BF16)
+
+    def window_places(i):
+        return [
             jnp.clip(pat_ref[i, j] - (SB * b - half), 0, SB + 2 * half - 1) for j in range(LSEL)
         ]
-        scores = scores_of(masked_queries(i), win_k, places)
-        kept = ml_v[i]
-        far_top, far_total = kept[:, :1], kept[:, HD : HD + 1]
-        top = jnp.maximum(jnp.max(scores, axis=1, keepdims=True), far_top)
-        raised = jnp.exp(scores - top)
-        shrink = jnp.exp(far_top - top)
-        inverse = 1.0 / (jnp.sum(raised, axis=1, keepdims=True) + far_total * shrink)
-        a_v[i] = by_head(mixed(raised.astype(BF16), win_v, places) * inverse)
-        c_v[i] = by_head(jnp.broadcast_to(shrink * inverse, (2 * BLK, PAIR)))
+
+    near_rows = LSEL * BLK
+
+    def window_scores(i, buffer):
+        scores = scores_of(i, win_k, window_places(i))
+        buffer[:near_rows] = scores
+        near_m[i, :8] = jnp.broadcast_to(jnp.max(scores, axis=0, keepdims=True), (8, 2 * BLK))
+
+    def window_mix(i, buffer, top):
+        weights = jnp.exp(buffer[:near_rows] - top).astype(BF16)
+        products, total = mixed(weights, win_v, window_places(i))
+        near_v[i] = jnp.concatenate(products, axis=0)
+        near_m[i, 8:] = jnp.broadcast_to(total, (8, 2 * BLK))
 
     def finish_block(i):
-        product = mixed(p_v[i], sum_v, summary_places(i))
-        return (a_v[i] + c_v[i] * by_head(product)).astype(BF16)
-
-    def weights_pair(t, carry):
-        summary_weights(2 * t)
-        summary_weights(2 * t + 1)
-
-        @pl.when(t < n_up[1])
-        def _():
-            relay(1, t)
-
-        @pl.when(t == 2)
-        def _():
-            for h in range(FIRST_SUM):
-                for kind in range(2):
-                    arrived(own_win((win_k, win_v)[kind], h), (k_recv, v_recv)[kind].at[h])
-                    halo_copy(kind, h).start()
-
-        return carry
-
-    lax.fori_loop(0, n_head, weights_pair, 0)
-
-    copy_below(1)
+        products, far_total = mixed(p_v[i], sum_v, summary_places(i))
+        far_top, near_top, near_total = m_v[i, :1], near_m[i, :1], near_m[i, 8:9]
+        top = jnp.maximum(far_top, near_top)
+        far, near = jnp.exp(far_top - top), jnp.exp(near_top - top)
+        inverse = 1.0 / (far_total * far + near_total * near)
+        far, near = far * inverse, near * inverse
+        rows = []
+        for which in range(2):
+            lanes = slice(which * BLK, (which + 1) * BLK)
+            near_part = near_v[i, which * HD : (which + 1) * HD]
+            rows.append(products[which] * far[:, lanes] + near_part * near[:, lanes])
+        return jnp.concatenate(rows, axis=0).T.astype(BF16)
+
     for kind in range(2):
         ref = (win_k, win_v)[kind]
         for h in range(FIRST_SUM):
@@ -341,12 +367,43 @@
             arrived(own_win(ref, FIRST_SUM + part), loc_sem.at[kind, part])
             arrived(ref.at[pl.ds(SUMB + 2 * part, 2)], loc_sem.at[kind, chunks + part])
 
+    n_query = 2 * n_head
+
+    def pipelined_pair(t, scores, use, tops):
+        first, second = 2 * t, 2 * t + 1
+        after = jnp.minimum(2 * t + 2, n_query - 1)
+        top = tops[first, :1]
+        scores(second, s_b)
+        use(first, s_a, top)
+        top = tops[second, :1]
+        scores(after, s_a)
+        use(second, s_b, top)
+
+    window_scores(0, s_a)
+
     def window_pair(t, carry):
-        window_block(2 * t)
-        window_block(2 * t + 1)
+        pipelined_pair(t, window_scores, window_mix, near_m)
+
+        @pl.when(t < chunks)
+        def _():
+            relay(0, n_up[0] - chunks + t)
+
+        @pl.when(t < n_up[1] + 2 * chunks - n_up[0])
+        def _():
+            relay(1, n_up[0] - 2 * chunks + t)
+
         return carry
 
     lax.fori_loop(0, n_head, window_pair, 0)
+    others(0)
+
+    summary_scores(0, s_a)
+
+    def weights_pair(t, carry):
+        pipelined_pair(t, summary_scores, summary_raise, m_v)
+        return carry
+
+    lax.fori_loop(0, n_head, weights_pair, 0)
     others(1)
 
     columns = pl.ds(pl.multiple_of(g * PAIR, PAIR), PAIR)
@@ -424,10 +481,12 @@
             blocks(SUMB * n_blk),
             blocks(SUMB * n_blk),
             blocks(n_query),
-            pltpu.VMEM((n_query, 2 * BLK, PAIR), F32),
-            pltpu.VMEM((n_query, 2 * BLK, SSEL * BLK), BF16),
-            pltpu.VMEM((n_query, BLK, PAIR), F32),
-            pltpu.VMEM((n_query, BLK, PAIR), F32),
+            pltpu.VMEM((n_query, 8, 2 * BLK), F32),
+            pltpu.VMEM((n_query, SSEL * BLK, 2 * BLK), BF16),
+            pltpu.VMEM((n_query, PAIR, BLK), F32),
+            pltpu.VMEM((n_query, 16, 2 * BLK), F32),
+            pltpu.VMEM((SSEL * BLK, 2 * BLK), F32),
+            pltpu.VMEM((SSEL * BLK, 2 * BLK), F32),
             pltpu.VMEM((rows, D), BF16),
             pltpu.VMEM((n_head, rows, PAIR), BF16),
             dma((3,)),
@@ -451,7 +510,7 @@
             dma((n_head,)),
         ],
         compiler_params=pltpu.CompilerParams(
-            collective_id=0, has_side_effects=True, vmem_limit_bytes=56 * 1024 * 1024
+            collective_id=0, has_side_effects=True, vmem_limit_bytes=53 * 1024 * 1024
         ),
     )(tokens[0], proj_weight, out_weight, pattern)
     return out.reshape(1, rows, D)

time: 79.4 us -> 69.8 us (0.88)
  Pallas kernels: 77.4 us -> 67.4 us
    pallas_call x1, Pallas kernels: 77.4 us -> 67.4 us  [on_device(): pl.pallas_call(functools.partial(kernel, n_head, n_blk), out_shape=jax.Sh...]
    unnamed x1 -> x3, local copies, waits for them, and re-layouts: 1.87 us -> 1.49 us
where the time goes in v3:
time: 69.8 us; the launch traced here: 68.9 us
  Pallas kernels  67.4 us (97%)
  local copies, waits for them, and re-layouts  1.49 us (2%)
    pallas_call x1, Pallas kernels, on_device(): pl.pallas_call(functools.partial(kernel, n_head, n_blk), out_shape=jax.Sh...  67.4 us
    unnamed x3, local copies, waits for them, and re-layouts  1.49 us

profile of v3, /device:TPU:6, one launch (start us, length us, event | category | flops | bytes accessed | tf_op | source)
XLA Modules:
  0.0 68.9 jit_solution(13227328062866259928)
XLA Ops:
  0.0 0.0 copy-start
  0.0 0.7 %copy-done = s32[16,16]{1,0:T(8,128)S(1)} copy-done((s32[16,16]{1,0:T(8,128)S(1)}, s32[16,16]{1,0:T(8,128)}, u32[]{:S(2)}) %copy-start) | copy-done | bytes 1048
  0.7 67.4 %shard_map.46 = bf16[256,1024]{1,0:T(8,128)(2,1)S(1)} custom-call(bf16[256,1024]{1,0:T(8,128)(2,1)} %bitcast.3, bf16[1024,3072]{1,0:T(8,128)(2,1)} %w_hbm.1, bf16[1024,1024]{1,0:T(8,128)(2,1)} %wo_hbm.1, s32[16,16]{1,0:T(8,128)S(1)} %copy-done), custom_call_target="tpu_custom_call" | custom-call | tf_op jit(solution)/shard_map/pallas_call | solution.py:466
  68.1 0.8 %copy.6 = bf16[1,256,1024]{2,1,0:T(8,128)(2,1)} copy(bf16[1,256,1024]{2,1,0:T(8,128)(2,1)S(1)} %bitcast.2) | data formatting | bytes 1048576
Async XLA Ops:
  0.0 0.7 %copy-start = (s32[16,16]{1,0:T(8,128)S(1)}, s32[16,16]{1,0:T(8,128)}, u32[]{:S(2)}) copy-start(s32[16,16]{1,0:T(8,128)} %pat_hbm.1) | copy-start | bytes 3076

commit v4 on v3

--- a/solution.py
+++ b/solution.py
@@ -208,12 +208,18 @@
     def _():
         send_all(qs, q_send, q_recv, own_q)
 
+    lag = 4
+
     def relays(n, carry):
         relay(0, n)
-        relay(1, n - chunks)
+
+        @pl.when(n >= lag)
+        def _():
+            relay(1, n - lag)
+
         return carry
 
-    lax.fori_loop(chunks, 2 * chunks, relays, 0)
+    lax.fori_loop(chunks, n_up[0], relays, 0)
 
     early = chunks * (1 - core)
 
@@ -281,9 +287,8 @@
         for kind in range(2):
             arrived(own_win((win_k, win_v)[kind], h), (k_recv, v_recv)[kind].at[h])
             halo_copy(kind, h).start()
-    lax.fori_loop(2 * chunks, n_up[0] - chunks, relays, 0)
-    for kind in range(2):
-        copy_below(kind)
+    copy_below(0)
+    others(0)
     for h in range(n_head):
         arrived(q_v.at[pl.ds(2 * h, 2)], q_recv.at[h])
     pat_copy.wait()
@@ -359,14 +364,6 @@
             rows.append(products[which] * far[:, lanes] + near_part * near[:, lanes])
         return jnp.concatenate(rows, axis=0).T.astype(BF16)
 
-    for kind in range(2):
-        ref = (win_k, win_v)[kind]
-        for h in range(FIRST_SUM):
-            arrived(halo_place(ref, h), halo_recv.at[kind, h])
-        for part in range(chunks):
-            arrived(own_win(ref, FIRST_SUM + part), loc_sem.at[kind, part])
-            arrived(ref.at[pl.ds(SUMB + 2 * part, 2)], loc_sem.at[kind, chunks + part])
-
     n_query = 2 * n_head
 
     def pipelined_pair(t, scores, use, tops):
@@ -379,31 +376,42 @@
         scores(after, s_a)
         use(second, s_b, top)
 
+    summary_scores(0, s_a)
+
+    def weights_pair(t, carry):
+        pipelined_pair(t, summary_scores, summary_raise, m_v)
+
+        @pl.when(t == 1)
+        def _():
+            relay(1, n_up[0] - lag + 0)
+
+        @pl.when(t == 3)
+        def _():
+            relay(1, n_up[0] - lag + 1)
+
+        @pl.when(t == 5)
+        def _():
+            relay(1, n_up[0] - lag + 2)
+
+        return carry
+
+    lax.fori_loop(0, n_head, weights_pair, 0)
+    copy_below(1)
+    for kind in range(2):
+        ref = (win_k, win_v)[kind]
+        for h in range(FIRST_SUM):
+            arrived(halo_place(ref, h), halo_recv.at[kind, h])
+        for part in range(chunks):
+            arrived(own_win(ref, FIRST_SUM + part), loc_sem.at[kind, part])
+            arrived(ref.at[pl.ds(SUMB + 2 * part, 2)], loc_sem.at[kind, chunks + part])
+
     window_scores(0, s_a)
 
     def window_pair(t, carry):
         pipelined_pair(t, window_scores, window_mix, near_m)
-
-        @pl.when(t < chunks)
-        def _():
-            relay(0, n_up[0] - chunks + t)
-
-        @pl.when(t < n_up[1] + 2 * chunks - n_up[0])
-        def _():
-            relay(1, n_up[0] - 2 * chunks + t)
-
         return carry
 
     lax.fori_loop(0, n_head, window_pair, 0)
-    others(0)
-
-    summary_scores(0, s_a)
-
-    def weights_pair(t, carry):
-        pipelined_pair(t, summary_scores, summary_raise, m_v)
-        return carry
-
-    lax.fori_loop(0, n_head, weights_pair, 0)
     others(1)
 
     columns = pl.ds(pl.multiple_of(g * PAIR, PAIR), PAIR)

time: 69.8 us -> 67.6 us (0.968); the launches traced: 68.9 us -> 67.5 us
  Pallas kernels: 67.4 us -> 66 us
    pallas_call x1, Pallas kernels: 67.4 us -> 66 us  [on_device(): pl.pallas_call(functools.partial(kernel, n_head, n_blk), out_shape=jax.Sh...]
where the time goes in v4:
time: 67.6 us; the launch traced here: 67.5 us
  Pallas kernels  66 us (98%)
  local copies, waits for them, and re-layouts  1.49 us (2%)
    pallas_call x1, Pallas kernels, on_device(): pl.pallas_call(functools.partial(kernel, n_head, n_blk), out_shape=jax.Sh...  66 us
    unnamed x3, local copies, waits for them, and re-layouts  1.49 us

profile of v4, /device:TPU:6, one launch (start us, length us, event | category | flops | bytes accessed | tf_op | source)
XLA Modules:
  0.0 67.5 jit_solution(13498162775042548677)
XLA Ops:
  0.0 0.0 copy-start
  0.0 0.7 %copy-done = s32[16,16]{1,0:T(8,128)S(1)} copy-done((s32[16,16]{1,0:T(8,128)S(1)}, s32[16,16]{1,0:T(8,128)}, u32[]{:S(2)}) %copy-start) | copy-done | bytes 1048
  0.7 66.0 %shard_map.46 = bf16[256,1024]{1,0:T(8,128)(2,1)S(1)} custom-call(bf16[256,1024]{1,0:T(8,128)(2,1)} %bitcast.3, bf16[1024,3072]{1,0:T(8,128)(2,1)} %w_hbm.1, bf16[1024,1024]{1,0:T(8,128)(2,1)} %wo_hbm.1, s32[16,16]{1,0:T(8,128)S(1)} %copy-done), custom_call_target="tpu_custom_call" | custom-call | tf_op jit(solution)/shard_map/pallas_call | solution.py:474
  66.7 0.8 %copy.6 = bf16[1,256,1024]{2,1,0:T(8,128)(2,1)} copy(bf16[1,256,1024]{2,1,0:T(8,128)(2,1)S(1)} %bitcast.2) | data formatting | bytes 1048576
Async XLA Ops:
  0.0 0.7 %copy-start = (s32[16,16]{1,0:T(8,128)S(1)}, s32[16,16]{1,0:T(8,128)}, u32[]{:S(2)}) copy-start(s32[16,16]{1,0:T(8,128)} %pat_hbm.1) | copy-start | bytes 3076

commit v5 on v4

--- a/solution.py
+++ b/solution.py
@@ -136,7 +136,8 @@
 
     @pl.when(jnp.logical_not(summary_owner))
     def _():
-        send_all(qs, q_send, q_recv, own_q)
+        send_all(ks, k_send, k_recv, own_win(win_k, g))
+        send_all(vs, v_send, v_recv, own_win(win_v, g))
 
     def piece(kind, source, part):
         return ks_kinds[kind].at[pl.ds(SUMB * source + 2 * part, 2)]
@@ -197,8 +198,7 @@
 
     @pl.when(jnp.logical_not(summary_owner))
     def _():
-        send_all(ks, k_send, k_recv, own_win(win_k, g))
-        send_all(vs, v_send, v_recv, own_win(win_v, g))
+        send_all(qs, q_send, q_recv, own_q)
 
     for n in range(chunks):
         relay(0, n)
@@ -219,7 +219,24 @@
 
         return carry
 
-    lax.fori_loop(chunks, n_up[0], relays, 0)
+    def halo_place(ref, h):
+        start = 3 * half + 2 * h if 2 * h < half else 2 * h - half
+        return ref.at[pl.ds(start, 2)]
+
+    def halo_copy(kind, h):
+        ref = (win_k, win_v)[kind]
+        shift = -1 if 2 * h < half else 1
+        return remote(
+            own_win(ref, h), halo_place(ref, h), halo_send.at[kind, h], halo_recv.at[kind, h],
+            blk=shifted(b, shift),
+        )
+
+    lax.fori_loop(chunks, 6, relays, 0)
+    for h in range(FIRST_SUM):
+        for kind in range(2):
+            arrived(own_win((win_k, win_v)[kind], h), (k_recv, v_recv)[kind].at[h])
+            halo_copy(kind, h).start()
+    lax.fori_loop(6, n_up[0], relays, 0)
 
     early = chunks * (1 - core)
 
@@ -271,22 +288,6 @@
 
         lax.fori_loop(0, chunks * n_blk // 2, body, 0)
 
-    def halo_place(ref, h):
-        start = 3 * half + 2 * h if 2 * h < half else 2 * h - half
-        return ref.at[pl.ds(start, 2)]
-
-    def halo_copy(kind, h):
-        ref = (win_k, win_v)[kind]
-        shift = -1 if 2 * h < half else 1
-        return remote(
-            own_win(ref, h), halo_place(ref, h), halo_send.at[kind, h], halo_recv.at[kind, h],
-            blk=shifted(b, shift),
-        )
-
-    for h in range(FIRST_SUM):
-        for kind in range(2):
-            arrived(own_win((win_k, win_v)[kind], h), (k_recv, v_recv)[kind].at[h])
-            halo_copy(kind, h).start()
     copy_below(0)
     others(0)
     for h in range(n_head):
@@ -414,14 +415,15 @@
     lax.fori_loop(0, n_head, window_pair, 0)
     others(1)
 
-    columns = pl.ds(pl.multiple_of(g * PAIR, PAIR), PAIR)
+    def out_dest(t):
+        return lax.rem(g + 2 * t + 1 - (n_head - 1) * (t // (n_head // 2)), n_head)
 
     def out_to(t):
-        dest = lax.rem(g + 1 + t, n_head)
-        return remote(ost.at[t], attn.at[:, columns], out_send.at[t], out_recv.at[g], head=dest)
+        dest = out_dest(t)
+        return remote(ost.at[t], attn.at[g], out_send.at[t], out_recv.at[g], head=dest)
 
     def finish_pair(t, carry):
-        dest = lax.rem(g + 1 + t, n_head)
+        dest = out_dest(t)
         ost[t, :BLK] = finish_block(2 * dest)
         ost[t, BLK:] = finish_block(2 * dest + 1)
 
@@ -432,12 +434,13 @@
         return carry
 
     lax.fori_loop(0, n_head, finish_pair, 0)
-    pltpu.make_async_copy(ost.at[n_head - 1], attn.at[:, columns], out_recv.at[g]).start()
+    pltpu.make_async_copy(ost.at[n_head - 1], attn.at[g], out_recv.at[g]).start()
 
     wo_copy.wait()
     for h in range(n_head):
-        arrived(attn.at[:, pl.ds(h * PAIR, PAIR)], out_recv.at[h])
-    out_ref[...] = jnp.dot(attn[...], wo_v[...], preferred_element_type=F32).astype(BF16)
+        arrived(attn.at[h], out_recv.at[h])
+    heads = jnp.concatenate([attn[h] for h in range(n_head)], axis=1)
+    out_ref[...] = jnp.dot(heads, wo_v[...], preferred_element_type=F32).astype(BF16)
 
     for k in range(1, n_head):
         exchange(ks, k_send, k_recv, k, own_q).wait_send()
@@ -495,7 +498,7 @@
             pltpu.VMEM((n_query, 16, 2 * BLK), F32),
             pltpu.VMEM((SSEL * BLK, 2 * BLK), F32),
             pltpu.VMEM((SSEL * BLK, 2 * BLK), F32),
-            pltpu.VMEM((rows, D), BF16),
+            pltpu.VMEM((n_head, rows, PAIR), BF16),
             pltpu.VMEM((n_head, rows, PAIR), BF16),
             dma((3,)),
             dma((n_head,)),

time: 67.6 us -> 66.6 us (0.985)
  Pallas kernels: 66 us -> 65 us
    pallas_call x1, Pallas kernels: 66 us -> 65 us  [on_device(): pl.pallas_call(functools.partial(kernel, n_head, n_blk), out_shape=jax.Sh...]
where the time goes in v5:
time: 66.6 us; the launch traced here: 66.5 us
  Pallas kernels  65 us (98%)
  local copies, waits for them, and re-layouts  1.49 us (2%)
    pallas_call x1, Pallas kernels, on_device(): pl.pallas_call(functools.partial(kernel, n_head, n_blk), out_shape=jax.Sh...  65 us
    unnamed x3, local copies, waits for them, and re-layouts  1.49 us

profile of v5, /device:TPU:6, one launch (start us, length us, event | category | flops | bytes accessed | tf_op | source)
XLA Modules:
  0.0 66.5 jit_solution(9492981497003669083)
XLA Ops:
  0.0 0.0 copy-start
  0.0 0.7 %copy-done = s32[16,16]{1,0:T(8,128)S(1)} copy-done((s32[16,16]{1,0:T(8,128)S(1)}, s32[16,16]{1,0:T(8,128)}, u32[]{:S(2)}) %copy-start) | copy-done | bytes 1048
  0.7 65.0 %shard_map.46 = bf16[256,1024]{1,0:T(8,128)(2,1)S(1)} custom-call(bf16[256,1024]{1,0:T(8,128)(2,1)} %bitcast.3, bf16[1024,3072]{1,0:T(8,128)(2,1)} %w_hbm.1, bf16[1024,1024]{1,0:T(8,128)(2,1)} %wo_hbm.1, s32[16,16]{1,0:T(8,128)S(1)} %copy-done), custom_call_target="tpu_custom_call" | custom-call | tf_op jit(solution)/shard_map/pallas_call | solution.py:477
  65.7 0.8 %copy.6 = bf16[1,256,1024]{2,1,0:T(8,128)(2,1)} copy(bf16[1,256,1024]{2,1,0:T(8,128)(2,1)S(1)} %bitcast.2) | data formatting | bytes 1048576
Async XLA Ops:
  0.0 0.7 %copy-start = (s32[16,16]{1,0:T(8,128)S(1)}, s32[16,16]{1,0:T(8,128)}, u32[]{:S(2)}) copy-start(s32[16,16]{1,0:T(8,128)} %pat_hbm.1) | copy-start | bytes 3076

commit v6 on v5

--- a/solution.py
+++ b/solution.py
@@ -418,27 +418,37 @@
     def out_dest(t):
         return lax.rem(g + 2 * t + 1 - (n_head - 1) * (t // (n_head // 2)), n_head)
 
-    def out_to(t):
+    def half_rows(u):
+        return pl.ds(u * BLK, BLK)
+
+    def out_to(t, u):
         dest = out_dest(t)
-        return remote(ost.at[t], attn.at[g], out_send.at[t], out_recv.at[g], head=dest)
+        return remote(
+            ost.at[t, half_rows(u)], attn.at[g, half_rows(u)],
+            out_send.at[2 * t + u], out_recv.at[2 * g + u], head=dest,
+        )
 
     def finish_pair(t, carry):
         dest = out_dest(t)
-        ost[t, :BLK] = finish_block(2 * dest)
-        ost[t, BLK:] = finish_block(2 * dest + 1)
-
-        @pl.when(t < n_head - 1)
-        def _():
-            out_to(t).start()
+        for u in range(2):
+            ost[t, u * BLK : (u + 1) * BLK] = finish_block(2 * dest + u)
+
+            @pl.when(t < n_head - 1)
+            def _(u=u):
+                out_to(t, u).start()
 
         return carry
 
     lax.fori_loop(0, n_head, finish_pair, 0)
-    pltpu.make_async_copy(ost.at[n_head - 1], attn.at[g], out_recv.at[g]).start()
+    for u in range(2):
+        pltpu.make_async_copy(
+            ost.at[n_head - 1, half_rows(u)], attn.at[g, half_rows(u)], out_recv.at[2 * g + u]
+        ).start()
 
     wo_copy.wait()
     for h in range(n_head):
-        arrived(attn.at[h], out_recv.at[h])
+        for u in range(2):
+            arrived(attn.at[h, half_rows(u)], out_recv.at[2 * h + u])
     heads = jnp.concatenate([attn[h] for h in range(n_head)], axis=1)
     out_ref[...] = jnp.dot(heads, wo_v[...], preferred_element_type=F32).astype(BF16)
 
@@ -446,7 +456,8 @@
         exchange(ks, k_send, k_recv, k, own_q).wait_send()
         exchange(vs, v_send, v_recv, k, own_q).wait_send()
         exchange(qs, q_send, q_recv, k, own_q).wait_send()
-        out_to(k - 1).wait_send()
+        for u in range(2):
+            out_to(k - 1, u).wait_send()
     for kind in range(2):
         for h in range(FIRST_SUM):
             halo_copy(kind, h).wait_send()
@@ -517,8 +528,8 @@
             dma((2, FIRST_SUM)),
             dma((2, FIRST_SUM)),
             dma((2, SUMB)),
-            dma((n_head,)),
-            dma((n_head,)),
+            dma((2 * n_head,)),
+            dma((2 * n_head,)),
         ],
         compiler_params=pltpu.CompilerParams(
             collective_id=0, has_side_effects=True, vmem_limit_bytes=53 * 1024 * 1024

time: 66.6 us -> 68 us (1.021)
  Pallas kernels: 65 us -> 66.3 us
    pallas_call x1, Pallas kernels: 65 us -> 66.3 us  [on_device(): pl.pallas_call(functools.partial(kernel, n_head, n_blk), out_shape=jax.Sh...]
where the time goes in v6:
time: 68 us; the launch traced here: 67.8 us
  Pallas kernels  66.3 us (98%)
  local copies, waits for them, and re-layouts  1.49 us (2%)
    pallas_call x1, Pallas kernels, on_device(): pl.pallas_call(functools.partial(kernel, n_head, n_blk), out_shape=jax.Sh...  66.3 us
    unnamed x3, local copies, waits for them, and re-layouts  1.49 us

profile of v6, /device:TPU:6, one launch (start us, length us, event | category | flops | bytes accessed | tf_op | source)
XLA Modules:
  0.0 67.8 jit_solution(4093069495782943261)
XLA Ops:
  0.0 0.0 copy-start
  0.0 0.7 %copy-done = s32[16,16]{1,0:T(8,128)S(1)} copy-done((s32[16,16]{1,0:T(8,128)S(1)}, s32[16,16]{1,0:T(8,128)}, u32[]{:S(2)}) %copy-start) | copy-done | bytes 1048
  0.7 66.3 %shard_map.46 = bf16[256,1024]{1,0:T(8,128)(2,1)S(1)} custom-call(bf16[256,1024]{1,0:T(8,128)(2,1)} %bitcast.3, bf16[1024,3072]{1,0:T(8,128)(2,1)} %w_hbm.1, bf16[1024,1024]{1,0:T(8,128)(2,1)} %wo_hbm.1, s32[16,16]{1,0:T(8,128)S(1)} %copy-done), custom_call_target="tpu_custom_call" | custom-call | tf_op jit(solution)/shard_map/pallas_call | solution.py:488
  67.0 0.8 %copy.6 = bf16[1,256,1024]{2,1,0:T(8,128)(2,1)} copy(bf16[1,256,1024]{2,1,0:T(8,128)(2,1)S(1)} %bitcast.2) | data formatting | bytes 1048576
Async XLA Ops:
  0.0 0.7 %copy-start = (s32[16,16]{1,0:T(8,128)S(1)}, s32[16,16]{1,0:T(8,128)}, u32[]{:S(2)}) copy-start(s32[16,16]{1,0:T(8,128)} %pat_hbm.1) | copy-start | bytes 3076
